TPU v7x, 32 devices: a whole 2x2x4 slice. The times are simulated.
32 devices in a mesh: ctx: 4 (over y, x), exp: 8 (over z, core).
Axes of the slice: x: 2, y: 2, z: 4, core: 2. Of those that a mesh axis runs over, the one named last changes fastest.
Arguments:
- queries: bfloat16 [512, 12288], P('ctx', 'exp'), may hold values from -40.35234 to 40.35234
- key_rows: bfloat16 [512, 12288], P('ctx', 'exp'), may hold values from -4 to 4
- value_rows: bfloat16 [512, 8192], P('ctx', 'exp'), may hold values from -6 to 6
- w_out: bfloat16 [8192, 3584], P('exp'), may hold values from -0.5 to 0.5
- residual: bfloat16 [512, 3584], P(('ctx', 'exp')), may hold values from -3 to 3
- norm_gain: float32 [3584], replicated, may hold values from 0.1 to 1.9
- router: bfloat16 [3584, 32], replicated, may hold values from -0.09375 to 0.09375
- routing: int32 [8, 4, 16, 8], P('exp'), may hold values from 0 to 31, all different within a row; in each aligned block of 64 rows (0 to 63, 64 to 127, ..., all dimensions but the last counted through in order) at most 24 rows name the same one
- w_gate: bfloat16 [32, 3584, 2048], P('exp', None, 'ctx'), may hold values from -0.09375 to 0.09375
- w_up: bfloat16 [32, 3584, 2048], P('exp', None, 'ctx'), may hold values from -0.09375 to 0.09375
- w_down: bfloat16 [32, 2048, 3584], P('exp', 'ctx'), may hold values from -0.125 to 0.125
Outputs:
- mixed: bfloat16 [512, 3584], P(('ctx', 'exp'))
Inputs may be any that keep to these rules, and one draw needn't show every extreme that they name: `routing`: each token lists 8 different experts. Among the 64 tokens at one index of the first dimension, no expert is listed more than 24 times, and in every draw some expert is listed exactly 24 times in some such group.
All inputs are finite; a program needn't handle non-finite values.
Results may differ from a plain program's by a relative error of at most 0.025.
Values may be sent and summed in bfloat16 or wider, within the bound.
A program may use at most 128 MiB of HBM per device.

v0:
```python
import jax
import jax.numpy as jnp
from jax import lax
from jax.sharding import PartitionSpec as P

DQK = 192
DV = 128
NEG = -1e30


def from_behind(block, axis, distance):
    devices = range(lax.axis_size(axis))
    route = [((i - distance) % len(devices), i) for i in devices]
    return lax.ppermute(block, axis, route)


def body(
    queries, key_rows, value_rows, w_out, residual, norm_gain, router, routing, w_gate, w_up, w_down
):
    ctx_index = lax.axis_index("ctx")
    ctx_count = lax.axis_size("ctx")
    tok_rows = queries.shape[0]
    heads_here = queries.shape[1] // DQK
    q_full = queries.reshape(tok_rows, heads_here, DQK)
    k_full = key_rows.reshape(tok_rows, heads_here, DQK)
    v_full = value_rows.reshape(tok_rows, heads_here, DV)
    positions = jnp.arange(tok_rows, dtype=jnp.int32)
    score_scale = DQK ** (-0.5)

    def attend(state, q_part, k_part, v_part, q_source, k_source):
        row_max, row_total, accum = state
        scores = (
            jnp.einsum("thd,shd->hts", q_part, k_part, preferred_element_type=jnp.float32)
            * score_scale
        )
        query_pos = q_source * tok_rows + positions
        key_pos = k_source * tok_rows + positions
        allowed = (key_pos[None, :] <= query_pos[:, None])[None]
        scores = jnp.where(allowed, scores, NEG)
        new_max = jnp.maximum(row_max, jnp.max(scores, axis=-1))
        probs = jnp.where(allowed, jnp.exp(scores - new_max[..., None]), 0.0)
        carry_scale = jnp.exp(row_max - new_max)
        row_total = row_total * carry_scale + jnp.sum(probs, axis=-1)
        accum = accum * carry_scale[..., None] + jnp.einsum(
            "hts,shd->htd", probs, v_part.astype(jnp.float32), precision=lax.Precision.HIGHEST
        )
        return (new_max, row_total, accum)

    def visit(state, q_part, k_part, v_part, q_source, k_source):
        return attend(state, q_part, k_part, v_part, q_source, k_source)

    home = visit(
        (
            jnp.full((heads_here, tok_rows), NEG, jnp.float32),
            jnp.zeros((heads_here, tok_rows), jnp.float32),
            jnp.zeros((heads_here, tok_rows, DV), jnp.float32),
        ),
        q_full,
        k_full,
        v_full,
        ctx_index,
        ctx_index,
    )

    def turn(turn_index, carry):
        state, k_now, v_now = carry
        k_now, v_now = from_behind((k_now, v_now), "ctx", -1)
        source = (ctx_index + turn_index + 1) % ctx_count
        state = visit(state, q_full, k_now, v_now, ctx_index, source)
        return (state, k_now, v_now)

    carried = lax.fori_loop(0, ctx_count - 1, turn, (home, k_full, v_full))
    row_total, accum = (carried[0][1], carried[0][2])
    final = accum / row_total[..., None]
    attended = final.transpose(1, 0, 2).reshape(tok_rows, heads_here * DV).astype(jnp.bfloat16)
    attn_out = lax.psum_scatter(
        jnp.dot(attended, w_out, preferred_element_type=jnp.float32).astype(jnp.bfloat16),
        "exp",
        scatter_dimension=0,
        tiled=True,
    ).astype(jnp.float32)
    hidden_state = residual.astype(jnp.float32) + attn_out
    mean_square = jnp.mean(hidden_state * hidden_state, axis=-1, keepdims=True)
    normed = (hidden_state * lax.rsqrt(mean_square + 1e-06) * norm_gain).astype(jnp.bfloat16)
    column = lax.all_gather(normed, "ctx", axis=0, tiled=True)
    experts = router.shape[1]
    top_count = routing.shape[-1]
    routes = routing.reshape(-1, top_count)
    group_rows = routes.shape[0]
    capacity = 3 * group_rows * top_count // (2 * experts)
    d_model = column.shape[1]
    affinity = jax.nn.sigmoid(jnp.dot(column, router, preferred_element_type=jnp.float32))
    onehot = routes[:, :, None] == jnp.arange(experts, dtype=jnp.int32)[None, None, :]
    chosen = jnp.sum(jnp.where(onehot, affinity[:, None, :], 0.0), axis=-1)
    route_weight = 2.5 * chosen / jnp.sum(chosen, axis=-1, keepdims=True)
    flat_hot = onehot.reshape(group_rows * top_count, experts).astype(jnp.int32)
    before = jnp.cumsum(flat_hot, axis=0) - flat_hot
    slot_index = jnp.sum(before * flat_hot, axis=-1)
    target = routes.reshape(-1) * capacity + slot_index
    matches = (target[:, None] == jnp.arange(experts * capacity, dtype=jnp.int32)[None, :]).reshape(
        group_rows, top_count, experts * capacity
    )
    dispatch_table = jnp.any(matches, axis=1).T.astype(jnp.bfloat16)
    outgoing = jnp.dot(dispatch_table, column, preferred_element_type=jnp.float32).astype(
        jnp.bfloat16
    )
    outgoing = outgoing.reshape(experts, capacity, d_model)
    arrived = lax.all_to_all(outgoing, "exp", split_axis=0, concat_axis=0, tiled=True)
    local_experts = w_gate.shape[0]
    sources = arrived.shape[0] // local_experts
    slots_here = arrived.shape[1]
    inputs = arrived.reshape(sources, local_experts, slots_here, d_model)
    gate = jnp.einsum("sexd,edf->sexf", inputs, w_gate, preferred_element_type=jnp.float32)
    upper = jnp.einsum("sexd,edf->sexf", inputs, w_up, preferred_element_type=jnp.float32)
    expert_hidden = (jax.nn.silu(gate) * upper).astype(jnp.bfloat16)
    partial_value = jnp.einsum(
        "sexf,efd->sexd", expert_hidden, w_down, preferred_element_type=jnp.float32
    ).astype(jnp.bfloat16)
    partial_value = partial_value.reshape(sources * local_experts, slots_here, d_model)
    returned = lax.all_to_all(partial_value, "exp", split_axis=0, concat_axis=0, tiled=True)
    flat_back = returned.reshape(experts * capacity, d_model)
    picked = (
        jnp.take(flat_back, target, axis=0)
        .reshape(group_rows, top_count, d_model)
        .astype(jnp.float32)
    )
    combined = jnp.sum(picked * route_weight[..., None], axis=1)
    moe_out = lax.psum_scatter(
        combined.astype(jnp.bfloat16), "ctx", scatter_dimension=0, tiled=True
    ).astype(jnp.float32)
    return (hidden_state + moe_out).astype(jnp.bfloat16)


def solution(mesh):
    in_specs = (
        P("ctx", "exp"),
        P("ctx", "exp"),
        P("ctx", "exp"),
        P("exp", None),
        P(("ctx", "exp"), None),
        P(),
        P(),
        P("exp", None, None, None),
        P("exp", None, "ctx"),
        P("exp", None, "ctx"),
        P("exp", "ctx", None),
    )
    out_specs = P(("ctx", "exp"), None)
    return jax.shard_map(body, mesh=mesh, in_specs=in_specs, out_specs=out_specs, check_vma=False)
```

profile of v0, /device:TPU:0, one launch (start us, length us, event | category | flops | bytes accessed | tf_op | source)
XLA Modules:
  0.0 447.0 jit_solution(17789973888606974906)
XLA Ops:
  6.6 1.1 copy.40
  7.8 0.2 copy.43
  8.0 1.2 copy.38
  9.2 1.2 copy.39
  10.4 0.4 fusion.46
  10.8 0.1 fusion.35
  10.9 0.6 convolution_add_fusion.1
  11.6 54.3 %while.25 = (s32[]{:T(128)}, f32[8,128]{1,0:T(8,128)S(1)}, f32[8,128]{1,0:T(8,128)S(1)}, f32[8,128,128]{2,1,0:T(8,128)S(1)}, bf16[128,8,192]{0,2,1:T(8,128)(2,1)...) while((s32[]{:T(128)}, f32[8,128]{1,0:T(8,128)S(1)}, ...), condition=%wide.region_5.6_spmd.clone.clone, body=%wide.region_2.5_spmd.clone.clone.sunk | while | flops 252987664 | bytes 7735662 | solution.py:72
  11.6 4.0 collective-permute-start
  15.6 0.5 collective-permute-start.1
  16.2 13.4 %collective-permute-done.1 = bf16[128,8,128]{2,0,1:T(8,128)(2,1)S(1)} collective-permute-done((bf16[128,8,128]{2,0,1:T(8,128)(2,1)S(1)}, bf16[128,8,128]{2,0,1:T(8,128)(2,1)S(1)}, u32[]{:S(2)}, u32[]{:S(2)}) %collective-permute-start.1) | collective-permute-done | bytes 262176 | tf_op jit(solution)/shard_map/while/body/eval_jaxpr/ppermute | solution.py:14
  29.6 0.4 fusion.68
  30.0 0.1 fusion.69
  30.1 0.8 convolution_add_fusion.3
  30.9 3.4 collective-permute-start
  34.5 13.0 %collective-permute-done.1 = bf16[128,8,128]{2,0,1:T(8,128)(2,1)S(1)} collective-permute-done((bf16[128,8,128]{2,0,1:T(8,128)(2,1)S(1)}, bf16[128,8,128]{2,0,1:T(8,128)(2,1)S(1)}, u32[]{:S(2)}, u32[]{:S(2)}) %collective-permute-start.1) | collective-permute-done | bytes 262176 | tf_op jit(solution)/shard_map/while/body/eval_jaxpr/ppermute | solution.py:14
  47.5 0.4 fusion.68
  47.9 0.1 fusion.69
  48.1 0.8 convolution_add_fusion.3
  48.8 3.4 collective-permute-start
  52.4 12.1 %collective-permute-done.1 = bf16[128,8,128]{2,0,1:T(8,128)(2,1)S(1)} collective-permute-done((bf16[128,8,128]{2,0,1:T(8,128)(2,1)S(1)}, bf16[128,8,128]{2,0,1:T(8,128)(2,1)S(1)}, u32[]{:S(2)}, u32[]{:S(2)}) %collective-permute-start.1) | collective-permute-done | bytes 262176 | tf_op jit(solution)/shard_map/while/body/eval_jaxpr/ppermute | solution.py:14
  64.6 0.4 fusion.68
  65.0 0.1 fusion.69
  65.1 0.8 convolution_add_fusion.3
  65.9 0.2 copy.44
  66.2 5.2 %convolution_convert_fusion.1 = bf16[128,3584]{1,0:T(8,128)(2,1)} fusion(bf16[128,1024]{0,1:T(8,128)(2,1)S(1)} %bitcast.110, bf16[1024,3584]{1,0:T(8,128)(2,1)} %param.16), kind=kOutput, calls=%fused_computation.28 | convolution fusion | flops 939982848 | bytes 8519680 | tf_op jit(solution)/shard_map/dot_general | solution.py:77
  71.8 1.2 reduce-window.6
  73.0 0.2 slice_reduce_fusion
  73.2 0.1 fusion.41
  73.6 0.5 fusion.26
  74.2 31.8 %reduce-scatter.3.cloned.1.call-done = bf16[16,3584]{1,0:T(8,128)(2,1)} async-done(((bf16[128,3584]{1,0:T(8,128)(2,1)}), bf16[16,3584]{1,0:T(8,128)(2,1)}) %reduce-scatter.3.cloned.1.call-update) | async-done | bytes 114704 | tf_op jit(solution)/shard_map/reduce_scatter | solution.py:76
  106.0 1.0 multiply_reduce_fusion.1
  107.0 1.0 multiply_convert_fusion
  108.0 9.8 %all_gather.3 = bf16[64,3584]{1,0:T(8,128)(2,1)S(1)} all-gather(bf16[16,3584]{1,0:T(8,128)(2,1)S(1)} %multiply_convert_fusion), channel_id=1, replica_groups=mesh['ctx'=4,'exp'=8] {'ctx'}, dimensions={0}, use_global_device_ids=true | all-gather | bytes 573440 | tf_op jit(solution)/shard_map/all_gather | solution.py:85
  117.8 1.6 convolution_convert_fusion
  119.4 124.6 %all_to_all.10 = bf16[32,24,3584]{2,1,0:T(8,128)(2,1)S(1)} all-to-all(bf16[32,24,3584]{2,1,0:T(8,128)(2,1)S(1)} %bitcast.102), channel_id=1, replica_groups=mesh['ctx'=4,'exp'=8] {'exp'}, dimensions={0} | all-to-all | bytes 11010048 | tf_op jit(solution)/shard_map/all_to_all | solution.py:108
  244.0 6.9 %fusion.12 = f32[4,8,24,512]{3,2,1,0:T(8,128)S(1)} fusion(bf16[4,3584,512]{2,1,0:T(8,128)(2,1)} %param.21, bf16[8,4,24,3584]{3,2,1,0:T(8,128)(2,1)S(1)} %bitcast.106), kind=kOutput, calls=%fused_computation.20 | convolution fusion | flops 2818572288 | bytes 21757952 | tf_op jit(solution)/shard_map/sexd,edf->sexf/dot_general | solution.py:113
  250.9 8.6 %fusion.22 = bf16[8,4,24,512]{3,2,0,1:T(8,128)(2,1)S(1)} fusion(f32[4,8,24,512]{3,2,1,0:T(8,128)S(1)} %fusion.12, bf16[4,3584,512]{2,1,0:T(8,128)(2,1)} %param.22, bf16[8,4,24,3584]{3,2,1,0:T(8,128)(2,1)S(1)} %bitcast.107), kind=kOutput, calls=%fused_computation.31 | convolution fusion | flops 2820931584 | bytes 22544384 | tf_op jit(solution)/shard_map/sexd,edf->sexf/dot_general | solution.py:114
  259.5 8.2 %fusion.17 = bf16[8,4,24,3584]{3,2,0,1:T(8,128)(2,1)S(1)} fusion(bf16[8,4,24,512]{3,2,0,1:T(8,128)(2,1)S(1)} %fusion.22, bf16[4,512,3584]{2,1,0:T(8,128)(2,1)} %param.23), kind=kOutput, calls=%fused_computation.25 | convolution fusion | flops 2821324800 | bytes 20971520 | tf_op jit(solution)/shard_map/sexf,efd->sexd/dot_general | solution.py:116
  267.7 3.0 copy.54
  270.7 4.7 %all-to-all-start.1 = ((bf16[32,24,3584]{2,1,0:T(8,128)(2,1)}), bf16[32,24,3584]{2,1,0:T(8,128)(2,1)}, u32[]{:S(2)}, u32[]{:S(2)}) async-start(bf16[32,24,3584]{2,1,0:T(8,128)(2,1)} %bitcast.103), calls=%async_computation.2 | async-start | bytes 11010048 | tf_op jit(solution)/shard_map/all_to_all | solution.py:120
  275.4 0.3 reduce-scatter.5.cloned.1.call-start
  276.0 0.3 fusion.34
  276.4 121.1 %all-to-all-done.1 = bf16[32,24,3584]{2,1,0:T(8,128)(2,1)} async-done(((bf16[32,24,3584]{2,1,0:T(8,128)(2,1)}), bf16[32,24,3584]{2,1,0:T(8,128)(2,1)}, u32[]{:S(2)}, u32[]{:S(2)}) %all-to-all-start.1) | async-done | bytes 5505056 | tf_op jit(solution)/shard_map/all_to_all | solution.py:120
  397.5 11.3 %gather_fusion = bf16[512,3584]{1,0:T(8,128)(2,1)} fusion(bf16[768,3584]{1,0:T(8,128)(2,1)} %bitcast.18, s32[1024]{0:T(1024)S(1)} %pad_clamp_fusion), kind=kCustom, calls=%fused_computation | custom fusion | bytes 7342080 | tf_op jit(solution)/shard_map/jit(_take)/gather | solution.py:123
  408.8 6.8 %multiply_reduce_fusion = bf16[64,3584]{1,0:T(8,128)(2,1)} fusion(bf16[512,3584]{1,0:T(8,128)(2,1)} %gather_fusion, f32[64,8]{1,0:T(8,128)S(1)} %copy.56, pred[64,8]{1,0:T(8,128)(4,1)S(1)} %copy.50), kind=kLoop, calls=%fused_computation.22 | loop fusion | flops 7110656 | bytes 4131328 | tf_op jit(solution)/shard_map/reduce_sum | solution.py:127
  415.6 23.0 %reduce-scatter.5.cloned.1.call-done = bf16[16,3584]{1,0:T(8,128)(2,1)} async-done(((bf16[64,3584]{1,0:T(8,128)(2,1)}), bf16[16,3584]{1,0:T(8,128)(2,1)}) %reduce-scatter.5.cloned.1.call-update) | async-done | bytes 114704 | tf_op jit(solution)/shard_map/reduce_scatter | solution.py:128
  438.5 1.6 add_convert_fusion
  (66 shorter events, 1.9 us)
Async XLA Ops:
  6.5 269.5 %copy-start = (bf16[3584,32]{0,1:T(8,128)(2,1)S(1)}, bf16[3584,32]{0,1:T(8,128)(2,1)}, u32[]{:S(2)}) copy-start(bf16[3584,32]{0,1:T(8,128)(2,1)} %param.19) | copy-start | bytes 688132
  6.5 99.4 %reduce-scatter.3.cloned.1.call-start = ((), (), s32[]{:S(2)}) async-start(), calls=%async_computation.4 | async-start | bytes 1032192 | tf_op jit(solution)/shard_map/reduce_scatter | solution.py:76
  11.6 18.0 %collective-permute-start = (bf16[128,8,192]{0,2,1:T(8,128)(2,1)S(1)}, bf16[128,8,192]{0,2,1:T(8,128)(2,1)S(1)}, u32[]{:S(2)}, u32[]{:S(2)}) collective-permute-start(bf16[128,8,192]{0,2,1:T(8,128)(2,1)S(1)} %get-tuple-element.417), channel_id=1, source_target_pairs={{8,0},{16,8},{24,16},{0,24},{9,1},{17,9},{25,17},{1,25},{10,2},{18... | collective-permute-start | bytes 1179656 | tf_op jit(solution)/shard_map/while/body/eval_jaxpr/ppermute | solution.py:14
  15.6 14.0 %collective-permute-start.1 = (bf16[128,8,128]{2,0,1:T(8,128)(2,1)S(1)}, bf16[128,8,128]{2,0,1:T(8,128)(2,1)S(1)}, u32[]{:S(2)}, u32[]{:S(2)}) collective-permute-start(bf16[128,8,128]{2,0,1:T(8,128)(2,1)S(1)} %get-tuple-element.418), channel_id=1, source_target_pairs={{8,0},{16,8},{24,16},{0,24},{9,1},{17,9},{25,17},{1,25},{10,2},{18... | collective-permute-start | bytes 786440 | tf_op jit(solution)/shard_map/while/body/eval_jaxpr/ppermute | solution.py:14
  30.9 16.6 %collective-permute-start = (bf16[128,8,192]{0,2,1:T(8,128)(2,1)S(1)}, bf16[128,8,192]{0,2,1:T(8,128)(2,1)S(1)}, u32[]{:S(2)}, u32[]{:S(2)}) collective-permute-start(bf16[128,8,192]{0,2,1:T(8,128)(2,1)S(1)} %get-tuple-element.417), channel_id=1, source_target_pairs={{8,0},{16,8},{24,16},{0,24},{9,1},{17,9},{25,17},{1,25},{10,2},{18... | collective-permute-start | bytes 1179656 | tf_op jit(solution)/shard_map/while/body/eval_jaxpr/ppermute | solution.py:14
  34.4 13.1 %collective-permute-start.1 = (bf16[128,8,128]{2,0,1:T(8,128)(2,1)S(1)}, bf16[128,8,128]{2,0,1:T(8,128)(2,1)S(1)}, u32[]{:S(2)}, u32[]{:S(2)}) collective-permute-start(bf16[128,8,128]{2,0,1:T(8,128)(2,1)S(1)} %get-tuple-element.418), channel_id=1, source_target_pairs={{8,0},{16,8},{24,16},{0,24},{9,1},{17,9},{25,17},{1,25},{10,2},{18... | collective-permute-start | bytes 786440 | tf_op jit(solution)/shard_map/while/body/eval_jaxpr/ppermute | solution.py:14
  48.8 15.7 %collective-permute-start = (bf16[128,8,192]{0,2,1:T(8,128)(2,1)S(1)}, bf16[128,8,192]{0,2,1:T(8,128)(2,1)S(1)}, u32[]{:S(2)}, u32[]{:S(2)}) collective-permute-start(bf16[128,8,192]{0,2,1:T(8,128)(2,1)S(1)} %get-tuple-element.417), channel_id=1, source_target_pairs={{8,0},{16,8},{24,16},{0,24},{9,1},{17,9},{25,17},{1,25},{10,2},{18... | collective-permute-start | bytes 1179656 | tf_op jit(solution)/shard_map/while/body/eval_jaxpr/ppermute | solution.py:14
  52.3 12.3 %collective-permute-start.1 = (bf16[128,8,128]{2,0,1:T(8,128)(2,1)S(1)}, bf16[128,8,128]{2,0,1:T(8,128)(2,1)S(1)}, u32[]{:S(2)}, u32[]{:S(2)}) collective-permute-start(bf16[128,8,128]{2,0,1:T(8,128)(2,1)S(1)} %get-tuple-element.418), channel_id=1, source_target_pairs={{8,0},{16,8},{24,16},{0,24},{9,1},{17,9},{25,17},{1,25},{10,2},{18... | collective-permute-start | bytes 786440 | tf_op jit(solution)/shard_map/while/body/eval_jaxpr/ppermute | solution.py:14
  66.2 5.3 %copy-start.3 = (s32[1,4,16,8]{2,3,1,0:T(8,128)S(1)}, s32[1,4,16,8]{2,3,1,0:T(8,128)}, u32[]{:S(2)}) copy-start(s32[1,4,16,8]{2,3,1,0:T(8,128)} %param.20) | copy-start | bytes 6148
  66.2 39.8 %copy-start.1 = (bf16[16,3584]{1,0:T(8,128)(2,1)S(1)}, bf16[16,3584]{1,0:T(8,128)(2,1)}, u32[]{:S(2)}) copy-start(bf16[16,3584]{1,0:T(8,128)(2,1)} %param.17) | copy-start | bytes 344068
  66.2 40.8 %copy-start.4 = (f32[3584]{0:T(1024)S(1)}, f32[3584]{0:T(1024)}, u32[]{:S(2)}) copy-start(f32[3584]{0:T(1024)} %param.18) | copy-start | bytes 43012
  270.7 126.7 %all-to-all-start.1 = ((bf16[32,24,3584]{2,1,0:T(8,128)(2,1)}), bf16[32,24,3584]{2,1,0:T(8,128)(2,1)}, u32[]{:S(2)}, u32[]{:S(2)}) async-start(bf16[32,24,3584]{2,1,0:T(8,128)(2,1)} %bitcast.103), calls=%async_computation.2 | async-start | bytes 11010048 | tf_op jit(solution)/shard_map/all_to_all | solution.py:120
  275.4 163.1 %reduce-scatter.5.cloned.1.call-start = ((), (), s32[]{:S(2)}) async-start(), calls=%async_computation.5 | async-start | bytes 573440 | tf_op jit(solution)/shard_map/reduce_scatter | solution.py:128
  397.5 41.1 %copy-start.2 = (bf16[16,3584]{1,0:T(8,128)(2,1)S(1)}, bf16[16,3584]{1,0:T(8,128)(2,1)}, u32[]{:S(2)}) copy-start(bf16[16,3584]{1,0:T(8,128)(2,1)} %reduce-scatter.3.cloned.1.call-done) | copy-start | bytes 344068
Sparse Core Ops, SparseCore 0:
  71.6 34.3 reduce-scatter.2
  415.7 22.7 reduce-scatter.4
where the time goes:
time: 447 us
  waiting for transfers between devices  214 us (48%)
  blocking collectives  134 us (30%)
  matrix products  35.1 us (8%)
  local copies, waits for them, and re-layouts  19.6 us (4%)
  starting transfers between devices  16.4 us (4%)
  between operations  13.7 us (3%)
  other arithmetic  13.3 us (3%)
    all_to_all x1, blocking collectives, body(): lax.all_to_all(outgoing, 'exp', split_axis=0, concat_axis=0, tiled=True)  125 us
    all_to_all x1, waiting for transfers between devices, body(): lax.all_to_all(partial_value, 'exp', split_axis=0, concat_axis=0, tiled=T...  121 us
    ppermute x6, waiting for transfers between devices, from_behind(): return lax.ppermute(block, axis, route)  38.4 us
    reduce_scatter x1, waiting for transfers between devices, body(): lax.psum_scatter(jnp.dot(attended, w_out, preferred_element_type=jnp.floa...  31.8 us
    reduce_scatter x1, waiting for transfers between devices, body(): lax.psum_scatter(combined.astype(jnp.bfloat16), 'ctx', scatter_dimension=...  23 us
    ppermute x6, starting transfers between devices, from_behind(): return lax.ppermute(block, axis, route)  11.5 us
    gather x1, local copies, waits for them, and re-layouts, body(): jnp.take(flat_back, target, axis=0).reshape(group_rows, top_count, d_model)  11.3 us
    all_gather x1, blocking collectives, body(): column = lax.all_gather(normed, 'ctx', axis=0, tiled=True)  9.75 us
  transfers between devices with their start and end apart: 9, of which 6 were waited for; matrix products, arithmetic and copies ran while one was open for 1% of the time, Pallas kernels for 0%

commit v1 on v0

--- a/solution.py
+++ b/solution.py
@@ -6,6 +6,22 @@
 DQK = 192
 DV = 128
 NEG = -1e30
+
+
+def swapped_with_each(shard, axis, split, join):
+    ways, here = (lax.axis_size(axis), lax.axis_index(axis))
+    width = shard.shape[split] // ways
+    shape = list(shard.shape)
+    shape[split] = width
+    height = shape[join]
+    shape[join] = height * ways
+    full = jnp.zeros(shape, shard.dtype)
+    for mask in range(ways):
+        part = lax.dynamic_slice_in_dim(shard, (here ^ mask) * width, width, axis=split)
+        if mask:
+            part = lax.ppermute(part, axis, [(d, d ^ mask) for d in range(ways)])
+        full = lax.dynamic_update_slice_in_dim(full, part, (here ^ mask) * height, axis=join)
+    return full
 
 
 def from_behind(block, axis, distance):
@@ -117,7 +133,7 @@
         "sexf,efd->sexd", expert_hidden, w_down, preferred_element_type=jnp.float32
     ).astype(jnp.bfloat16)
     partial_value = partial_value.reshape(sources * local_experts, slots_here, d_model)
-    returned = lax.all_to_all(partial_value, "exp", split_axis=0, concat_axis=0, tiled=True)
+    returned = swapped_with_each(partial_value, "exp", 0, 0)
     flat_back = returned.reshape(experts * capacity, d_model)
     picked = (
         jnp.take(flat_back, target, axis=0)

time: 447 us -> 459 us (1.027)
  blocking collectives: 134 us -> 9.75 us
  waiting for transfers between devices: 214 us -> 328 us
  local copies, waits for them, and re-layouts: 19.6 us -> 29 us
  matrix products: 35.1 us -> 41 us
  starting transfers between devices: 16.4 us -> 22 us
    all_to_all x1 -> x0, blocking collectives: 125 us -> none  [body(): lax.all_to_all(outgoing, 'exp', split_axis=0, concat_axis=0, tiled=True)]
    ppermute x0 -> x7, waiting for transfers between devices: none -> 114 us  [swapped_with_each(): part = lax.ppermute(part, axis, [(d, d ^ mask) for d in range(ways)])]
    dynamic_update_slice x0 -> x7, local copies, waits for them, and re-layouts: none -> 6.35 us  [swapped_with_each(): lax.dynamic_update_slice_in_dim(full, part, (here ^ mask) * height, axis=...]
    ppermute x0 -> x7, starting transfers between devices: none -> 5.63 us  [swapped_with_each(): part = lax.ppermute(part, axis, [(d, d ^ mask) for d in range(ways)])]
  transfers between devices with their start and end apart: 9 -> 16, of which waited for: 6 -> 9; matrix products, arithmetic and copies ran while one was open for 1% -> 2% of each run, Pallas kernels for 0% -> 0%
where the time goes in v1:
time: 459 us; the launch traced here: 458 us
  waiting for transfers between devices  328 us (71%)
  matrix products  41 us (9%)
  local copies, waits for them, and re-layouts  29 us (6%)
  starting transfers between devices  22 us (5%)
  other arithmetic  13.9 us (3%)
  between operations  13.7 us (3%)
  blocking collectives  9.75 us (2%)
    all_to_all x1, waiting for transfers between devices, body(): lax.all_to_all(outgoing, 'exp', split_axis=0, concat_axis=0, tiled=True)  121 us
    ppermute x7, waiting for transfers between devices, swapped_with_each(): part = lax.ppermute(part, axis, [(d, d ^ mask) for d in range(ways)])  114 us
    ppermute x6, waiting for transfers between devices, from_behind(): return lax.ppermute(block, axis, route)  38.4 us
    reduce_scatter x1, waiting for transfers between devices, body(): lax.psum_scatter(jnp.dot(attended, w_out, preferred_element_type=jnp.floa...  31.8 us
    reduce_scatter x1, waiting for transfers between devices, body(): lax.psum_scatter(combined.astype(jnp.bfloat16), 'ctx', scatter_dimension=...  23.1 us
    gather x1, local copies, waits for them, and re-layouts, body(): jnp.take(flat_back, target, axis=0).reshape(group_rows, top_count, d_model)  11.5 us
    ppermute x6, starting transfers between devices, from_behind(): return lax.ppermute(block, axis, route)  11.5 us
    dot_general x1, matrix products, body(): jnp.einsum('sexd,edf->sexf', inputs, w_up, preferred_element_type=jnp.flo...  10.1 us
  transfers between devices with their start and end apart: 16, of which 9 were waited for; matrix products, arithmetic and copies ran while one was open for 2% of the time, Pallas kernels for 0%

profile of v1, /device:TPU:0, one launch (start us, length us, event | category | flops | bytes accessed | tf_op | source)
XLA Modules:
  0.0 458.0 jit_solution(1757959039037953673)
XLA Ops:
  6.6 1.1 copy.40
  8.0 1.2 copy.38
  9.2 1.2 copy.39
  10.9 0.6 convolution_add_fusion.1
  11.6 54.3 %while.25 = (s32[]{:T(128)}, f32[8,128]{1,0:T(8,128)S(1)}, f32[8,128]{1,0:T(8,128)S(1)}, f32[8,128,128]{2,1,0:T(8,128)S(1)}, bf16[128,8,192]{0,2,1:T(8,128)(2,1)...) while((s32[]{:T(128)}, f32[8,128]{1,0:T(8,128)S(1)}, ...), condition=%wide.region_5.6_spmd.clone.clone, body=%wide.region_2.5_spmd.clone.clone.sunk | while | flops 252987664 | bytes 7735662 | solution.py:88
  11.6 4.0 collective-permute-start
  16.2 13.4 %collective-permute-done.1 = bf16[128,8,128]{2,0,1:T(8,128)(2,1)S(1)} collective-permute-done((bf16[128,8,128]{2,0,1:T(8,128)(2,1)S(1)}, bf16[128,8,128]{2,0,1:T(8,128)(2,1)S(1)}, u32[]{:S(2)}, u32[]{:S(2)}) %collective-permute-start.1) | collective-permute-done | bytes 262176 | tf_op jit(solution)/shard_map/while/body/eval_jaxpr/ppermute | solution.py:30
  30.1 0.8 convolution_add_fusion.3
  30.9 3.4 collective-permute-start
  34.5 13.0 %collective-permute-done.1 = bf16[128,8,128]{2,0,1:T(8,128)(2,1)S(1)} collective-permute-done((bf16[128,8,128]{2,0,1:T(8,128)(2,1)S(1)}, bf16[128,8,128]{2,0,1:T(8,128)(2,1)S(1)}, u32[]{:S(2)}, u32[]{:S(2)}) %collective-permute-start.1) | collective-permute-done | bytes 262176 | tf_op jit(solution)/shard_map/while/body/eval_jaxpr/ppermute | solution.py:30
  48.1 0.8 convolution_add_fusion.3
  48.8 3.4 collective-permute-start
  52.4 12.1 %collective-permute-done.1 = bf16[128,8,128]{2,0,1:T(8,128)(2,1)S(1)} collective-permute-done((bf16[128,8,128]{2,0,1:T(8,128)(2,1)S(1)}, bf16[128,8,128]{2,0,1:T(8,128)(2,1)S(1)}, u32[]{:S(2)}, u32[]{:S(2)}) %collective-permute-start.1) | collective-permute-done | bytes 262176 | tf_op jit(solution)/shard_map/while/body/eval_jaxpr/ppermute | solution.py:30
  65.1 0.8 convolution_add_fusion.3
  66.2 5.2 %convolution_convert_fusion.1 = bf16[128,3584]{1,0:T(8,128)(2,1)} fusion(bf16[128,1024]{0,1:T(8,128)(2,1)S(1)} %bitcast.108, bf16[1024,3584]{1,0:T(8,128)(2,1)} %param.16), kind=kOutput, calls=%fused_computation.28 | convolution fusion | flops 939982848 | bytes 8519680 | tf_op jit(solution)/shard_map/dot_general | solution.py:93
  71.8 1.2 reduce-window.6
  73.6 0.5 fusion.26
  74.2 31.8 %reduce-scatter.3.cloned.1.call-done = bf16[16,3584]{1,0:T(8,128)(2,1)} async-done(((bf16[128,3584]{1,0:T(8,128)(2,1)}), bf16[16,3584]{1,0:T(8,128)(2,1)}) %reduce-scatter.3.cloned.1.call-update) | async-done | bytes 114704 | tf_op jit(solution)/shard_map/reduce_scatter | solution.py:92
  106.0 1.0 multiply_reduce_fusion.1
  107.0 1.0 multiply_convert_fusion
  108.0 9.8 %all_gather.3 = bf16[64,3584]{1,0:T(8,128)(2,1)S(1)} all-gather(bf16[16,3584]{1,0:T(8,128)(2,1)S(1)} %multiply_convert_fusion), channel_id=1, replica_groups=mesh['ctx'=4,'exp'=8] {'ctx'}, dimensions={0}, use_global_device_ids=true | all-gather | bytes 573440 | tf_op jit(solution)/shard_map/all_gather | solution.py:101
  117.8 4.1 convolution_convert_fusion
  121.9 4.7 %all-to-all-start = ((bf16[32,24,3584]{2,1,0:T(8,128)(2,1)}), bf16[32,24,3584]{2,1,0:T(8,128)(2,1)}, u32[]{:S(2)}, u32[]{:S(2)}) async-start(bf16[32,24,3584]{2,1,0:T(8,128)(2,1)} %bitcast.102), calls=%async_computation.1 | async-start | bytes 11010048 | tf_op jit(solution)/shard_map/all_to_all | solution.py:124
  127.0 0.7 copy.50
  127.7 120.9 %all-to-all-done = bf16[32,24,3584]{2,1,0:T(8,128)(2,1)} async-done(((bf16[32,24,3584]{2,1,0:T(8,128)(2,1)}), bf16[32,24,3584]{2,1,0:T(8,128)(2,1)}, u32[]{:S(2)}, u32[]{:S(2)}) %all-to-all-start) | async-done | bytes 5505056 | tf_op jit(solution)/shard_map/all_to_all | solution.py:124
  248.6 8.8 %fusion.12 = f32[4,8,24,512]{3,2,1,0:T(8,128)S(1)} fusion(bf16[4,3584,512]{2,1,0:T(8,128)(2,1)} %param.21, bf16[8,4,24,3584]{3,2,1,0:T(8,128)(2,1)} %bitcast.7), kind=kOutput, calls=%fused_computation.20 | convolution fusion | flops 2818572288 | bytes 21757952 | tf_op jit(solution)/shard_map/sexd,edf->sexf/dot_general | solution.py:129
  257.4 10.1 %fusion.22 = bf16[8,4,24,512]{3,2,0,1:T(8,128)(2,1)S(1)} fusion(f32[4,8,24,512]{3,2,1,0:T(8,128)S(1)} %fusion.12, bf16[4,3584,512]{2,1,0:T(8,128)(2,1)} %param.22, bf16[8,4,24,3584]{3,2,1,0:T(8,128)(2,1)} %bitcast.7), kind=kOutput, calls=%fused_computation.31 | convolution fusion | flops 2820931584 | bytes 22544384 | tf_op jit(solution)/shard_map/sexd,edf->sexf/dot_general | solution.py:130
  267.5 8.2 %fusion.17 = bf16[8,4,24,3584]{3,2,0,1:T(8,128)(2,1)S(1)} fusion(bf16[8,4,24,512]{3,2,0,1:T(8,128)(2,1)S(1)} %fusion.22, bf16[4,512,3584]{2,1,0:T(8,128)(2,1)} %param.23), kind=kOutput, calls=%fused_computation.25 | convolution fusion | flops 2821324800 | bytes 20971520 | tf_op jit(solution)/shard_map/sexf,efd->sexd/dot_general | solution.py:132
  276.3 2.7 broadcast_in_dim.127
  279.0 2.0 constant_dynamic-slice_fusion
  281.0 0.6 pad_clamp_fusion
  282.1 1.5 collective-permute-start.8
  283.6 2.5 collective-permute-start.7
  286.1 1.6 collective-permute-start.4
  287.7 0.9 constant_dynamic-update-slice_fusion.6
  288.6 41.4 %collective-permute-done.3 = bf16[4,24,3584]{2,1,0:T(8,128)(2,1)S(1)} collective-permute-done((bf16[4,24,3584]{2,1,0:T(8,128)(2,1)}, bf16[4,24,3584]{2,1,0:T(8,128)(2,1)S(1)}, u32[]{:S(2)}, u32[]{:S(2)}) %collective-permute-start.3) | collective-permute-done | bytes 688160 | tf_op jit(solution)/shard_map/ppermute | solution.py:22
  330.0 0.9 constant_dynamic-update-slice_fusion.5
  331.0 26.2 %collective-permute-done.4 = bf16[4,24,3584]{2,1,0:T(8,128)(2,1)S(1)} collective-permute-done((bf16[4,24,3584]{2,1,0:T(8,128)(2,1)}, bf16[4,24,3584]{2,1,0:T(8,128)(2,1)S(1)}, u32[]{:S(2)}, u32[]{:S(2)}) %collective-permute-start.4) | collective-permute-done | bytes 688160 | tf_op jit(solution)/shard_map/ppermute | solution.py:22
  357.2 0.9 constant_dynamic-update-slice_fusion.4
  358.1 46.5 %collective-permute-done.5 = bf16[4,24,3584]{2,1,0:T(8,128)(2,1)S(1)} collective-permute-done((bf16[4,24,3584]{2,1,0:T(8,128)(2,1)}, bf16[4,24,3584]{2,1,0:T(8,128)(2,1)S(1)}, u32[]{:S(2)}, u32[]{:S(2)}) %collective-permute-start.5) | collective-permute-done | bytes 688160 | tf_op jit(solution)/shard_map/ppermute | solution.py:22
  404.6 0.9 constant_dynamic-update-slice_fusion.3
  405.5 0.9 constant_dynamic-update-slice_fusion.2
  406.4 0.9 constant_dynamic-update-slice_fusion.1
  407.3 0.9 constant_dynamic-update-slice_fusion
  408.2 11.5 %gather_fusion = bf16[512,3584]{1,0:T(8,128)(2,1)} fusion(bf16[768,3584]{1,0:T(8,128)(2,1)} %bitcast.18, s32[1024]{0:T(1024)S(1)} %copy-done.6), kind=kCustom, calls=%fused_computation | custom fusion | bytes 7342080 | tf_op jit(solution)/shard_map/jit(_take)/gather | solution.py:139
  419.7 6.8 %multiply_reduce_fusion = bf16[64,3584]{1,0:T(8,128)(2,1)} fusion(bf16[512,3584]{1,0:T(8,128)(2,1)} %gather_fusion, f32[64,8]{1,0:T(8,128)S(1)} %copy.56, pred[64,8]{1,0:T(8,128)(4,1)S(1)} %copy-done.4), kind=kLoop, calls=%fused_computation.22 | loop fusion | flops 7110656 | bytes 4131328 | tf_op jit(solution)/shard_map/reduce_sum | solution.py:143
  426.5 23.1 %reduce-scatter.5.cloned.1.call-done = bf16[16,3584]{1,0:T(8,128)(2,1)} async-done(((bf16[64,3584]{1,0:T(8,128)(2,1)}), bf16[16,3584]{1,0:T(8,128)(2,1)}) %reduce-scatter.5.cloned.1.call-update) | async-done | bytes 114704 | tf_op jit(solution)/shard_map/reduce_scatter | solution.py:144
  449.6 1.6 add_convert_fusion
  (92 shorter events, 6.0 us)
Async XLA Ops:
  6.5 275.1 %copy-start = (bf16[3584,32]{0,1:T(8,128)(2,1)S(1)}, bf16[3584,32]{0,1:T(8,128)(2,1)}, u32[]{:S(2)}) copy-start(bf16[3584,32]{0,1:T(8,128)(2,1)} %param.19) | copy-start | bytes 688132
  6.5 99.4 %reduce-scatter.3.cloned.1.call-start = ((), (), s32[]{:S(2)}) async-start(), calls=%async_computation.3 | async-start | bytes 1032192 | tf_op jit(solution)/shard_map/reduce_scatter | solution.py:92
  11.6 18.0 %collective-permute-start = (bf16[128,8,192]{0,2,1:T(8,128)(2,1)S(1)}, bf16[128,8,192]{0,2,1:T(8,128)(2,1)S(1)}, u32[]{:S(2)}, u32[]{:S(2)}) collective-permute-start(bf16[128,8,192]{0,2,1:T(8,128)(2,1)S(1)} %get-tuple-element.425), channel_id=1, source_target_pairs={{8,0},{16,8},{24,16},{0,24},{9,1},{17,9},{25,17},{1,25},{10,2},{18... | collective-permute-start | bytes 1179656 | tf_op jit(solution)/shard_map/while/body/eval_jaxpr/ppermute | solution.py:30
  15.6 14.0 %collective-permute-start.1 = (bf16[128,8,128]{2,0,1:T(8,128)(2,1)S(1)}, bf16[128,8,128]{2,0,1:T(8,128)(2,1)S(1)}, u32[]{:S(2)}, u32[]{:S(2)}) collective-permute-start(bf16[128,8,128]{2,0,1:T(8,128)(2,1)S(1)} %get-tuple-element.426), channel_id=1, source_target_pairs={{8,0},{16,8},{24,16},{0,24},{9,1},{17,9},{25,17},{1,25},{10,2},{18... | collective-permute-start | bytes 786440 | tf_op jit(solution)/shard_map/while/body/eval_jaxpr/ppermute | solution.py:30
  30.9 16.6 %collective-permute-start = (bf16[128,8,192]{0,2,1:T(8,128)(2,1)S(1)}, bf16[128,8,192]{0,2,1:T(8,128)(2,1)S(1)}, u32[]{:S(2)}, u32[]{:S(2)}) collective-permute-start(bf16[128,8,192]{0,2,1:T(8,128)(2,1)S(1)} %get-tuple-element.425), channel_id=1, source_target_pairs={{8,0},{16,8},{24,16},{0,24},{9,1},{17,9},{25,17},{1,25},{10,2},{18... | collective-permute-start | bytes 1179656 | tf_op jit(solution)/shard_map/while/body/eval_jaxpr/ppermute | solution.py:30
  34.4 13.1 %collective-permute-start.1 = (bf16[128,8,128]{2,0,1:T(8,128)(2,1)S(1)}, bf16[128,8,128]{2,0,1:T(8,128)(2,1)S(1)}, u32[]{:S(2)}, u32[]{:S(2)}) collective-permute-start(bf16[128,8,128]{2,0,1:T(8,128)(2,1)S(1)} %get-tuple-element.426), channel_id=1, source_target_pairs={{8,0},{16,8},{24,16},{0,24},{9,1},{17,9},{25,17},{1,25},{10,2},{18... | collective-permute-start | bytes 786440 | tf_op jit(solution)/shard_map/while/body/eval_jaxpr/ppermute | solution.py:30
  48.8 15.7 %collective-permute-start = (bf16[128,8,192]{0,2,1:T(8,128)(2,1)S(1)}, bf16[128,8,192]{0,2,1:T(8,128)(2,1)S(1)}, u32[]{:S(2)}, u32[]{:S(2)}) collective-permute-start(bf16[128,8,192]{0,2,1:T(8,128)(2,1)S(1)} %get-tuple-element.425), channel_id=1, source_target_pairs={{8,0},{16,8},{24,16},{0,24},{9,1},{17,9},{25,17},{1,25},{10,2},{18... | collective-permute-start | bytes 1179656 | tf_op jit(solution)/shard_map/while/body/eval_jaxpr/ppermute | solution.py:30
  52.3 12.3 %collective-permute-start.1 = (bf16[128,8,128]{2,0,1:T(8,128)(2,1)S(1)}, bf16[128,8,128]{2,0,1:T(8,128)(2,1)S(1)}, u32[]{:S(2)}, u32[]{:S(2)}) collective-permute-start(bf16[128,8,128]{2,0,1:T(8,128)(2,1)S(1)} %get-tuple-element.426), channel_id=1, source_target_pairs={{8,0},{16,8},{24,16},{0,24},{9,1},{17,9},{25,17},{1,25},{10,2},{18... | collective-permute-start | bytes 786440 | tf_op jit(solution)/shard_map/while/body/eval_jaxpr/ppermute | solution.py:30
  66.2 5.3 %copy-start.3 = (s32[1,4,16,8]{2,3,1,0:T(8,128)S(1)}, s32[1,4,16,8]{2,3,1,0:T(8,128)}, u32[]{:S(2)}) copy-start(s32[1,4,16,8]{2,3,1,0:T(8,128)} %param.20) | copy-start | bytes 6148
  66.2 39.8 %copy-start.1 = (bf16[16,3584]{1,0:T(8,128)(2,1)S(1)}, bf16[16,3584]{1,0:T(8,128)(2,1)}, u32[]{:S(2)}) copy-start(bf16[16,3584]{1,0:T(8,128)(2,1)} %param.17) | copy-start | bytes 344068
  66.2 40.8 %copy-start.5 = (f32[3584]{0:T(1024)S(1)}, f32[3584]{0:T(1024)}, u32[]{:S(2)}) copy-start(f32[3584]{0:T(1024)} %param.18) | copy-start | bytes 43012
  121.9 126.7 %all-to-all-start = ((bf16[32,24,3584]{2,1,0:T(8,128)(2,1)}), bf16[32,24,3584]{2,1,0:T(8,128)(2,1)}, u32[]{:S(2)}, u32[]{:S(2)}) async-start(bf16[32,24,3584]{2,1,0:T(8,128)(2,1)} %bitcast.102), calls=%async_computation.1 | async-start | bytes 11010048 | tf_op jit(solution)/shard_map/all_to_all | solution.py:124
  126.6 323.1 %reduce-scatter.5.cloned.1.call-start = ((), (), s32[]{:S(2)}) async-start(), calls=%async_computation.4 | async-start | bytes 573440 | tf_op jit(solution)/shard_map/reduce_scatter | solution.py:144
  281.0 5.1 %collective-permute-start.2 = (bf16[4,24,3584]{2,1,0:T(8,128)(2,1)}, bf16[4,24,3584]{2,1,0:T(8,128)(2,1)S(1)}, u32[]{:S(2)}, u32[]{:S(2)}) collective-permute-start(bf16[4,24,3584]{2,1,0:T(8,128)(2,1)} %get-tuple-element.334), channel_id=1, source_target_pairs={{0,1},{1,0},{2,3},{3,2},{4,5},{5,4},{6,7},{7,6},{8,9},{9,8},{10,11... | collective-permute-start | bytes 2064392 | tf_op jit(solution)/shard_map/ppermute | solution.py:22
  281.9 126.3 %copy-start.6 = (s32[1024]{0:T(1024)S(1)}, s32[1024]{0:T(1024)}, u32[]{:S(2)}) copy-start(s32[1024]{0:T(1024)} %pad_clamp_fusion) | copy-start | bytes 12292
  282.0 48.1 %collective-permute-start.3 = (bf16[4,24,3584]{2,1,0:T(8,128)(2,1)}, bf16[4,24,3584]{2,1,0:T(8,128)(2,1)S(1)}, u32[]{:S(2)}, u32[]{:S(2)}) collective-permute-start(bf16[4,24,3584]{2,1,0:T(8,128)(2,1)} %get-tuple-element.333), channel_id=1, source_target_pairs={{0,2},{1,3},{2,0},{3,1},{4,6},{5,7},{6,4},{7,5},{8,10},{9,11},{10,... | collective-permute-start | bytes 2064392 | tf_op jit(solution)/shard_map/ppermute | solution.py:22
  282.1 125.2 %collective-permute-start.8 = (bf16[4,24,3584]{2,1,0:T(8,128)(2,1)S(1)}, bf16[4,24,3584]{2,1,0:T(8,128)(2,1)S(1)}, u32[]{:S(2)}, u32[]{:S(2)}) collective-permute-start(bf16[4,24,3584]{2,1,0:T(8,128)(2,1)S(1)} %get-tuple-element.328), channel_id=1, source_target_pairs={{0,7},{1,6},{2,5},{3,4},{4,3},{5,2},{6,1},{7,0},{8,15},{9,14},{10,... | collective-permute-start | bytes 2064392 | tf_op jit(solution)/shard_map/ppermute | solution.py:22
  283.6 122.8 %collective-permute-start.7 = (bf16[4,24,3584]{2,1,0:T(8,128)(2,1)S(1)}, bf16[4,24,3584]{2,1,0:T(8,128)(2,1)S(1)}, u32[]{:S(2)}, u32[]{:S(2)}) collective-permute-start(bf16[4,24,3584]{2,1,0:T(8,128)(2,1)S(1)} %get-tuple-element.329), channel_id=1, source_target_pairs={{0,6},{1,7},{2,4},{3,5},{4,2},{5,3},{6,0},{7,1},{8,14},{9,15},{10,... | collective-permute-start | bytes 2064392 | tf_op jit(solution)/shard_map/ppermute | solution.py:22
  286.1 119.4 %collective-permute-start.6 = (bf16[4,24,3584]{2,1,0:T(8,128)(2,1)}, bf16[4,24,3584]{2,1,0:T(8,128)(2,1)S(1)}, u32[]{:S(2)}, u32[]{:S(2)}) collective-permute-start(bf16[4,24,3584]{2,1,0:T(8,128)(2,1)} %get-tuple-element.330), channel_id=1, source_target_pairs={{0,5},{1,4},{2,7},{3,6},{4,1},{5,0},{6,3},{7,2},{8,13},{9,12},{10,... | collective-permute-start | bytes 2064392 | tf_op jit(solution)/shard_map/ppermute | solution.py:22
  286.1 71.1 %collective-permute-start.4 = (bf16[4,24,3584]{2,1,0:T(8,128)(2,1)}, bf16[4,24,3584]{2,1,0:T(8,128)(2,1)S(1)}, u32[]{:S(2)}, u32[]{:S(2)}) collective-permute-start(bf16[4,24,3584]{2,1,0:T(8,128)(2,1)} %get-tuple-element.332), channel_id=1, source_target_pairs={{0,3},{1,2},{2,1},{3,0},{4,7},{5,6},{6,5},{7,4},{8,11},{9,10},{10,... | collective-permute-start | bytes 2064392 | tf_op jit(solution)/shard_map/ppermute | solution.py:22
  330.0 74.5 %collective-permute-start.5 = (bf16[4,24,3584]{2,1,0:T(8,128)(2,1)}, bf16[4,24,3584]{2,1,0:T(8,128)(2,1)S(1)}, u32[]{:S(2)}, u32[]{:S(2)}) collective-permute-start(bf16[4,24,3584]{2,1,0:T(8,128)(2,1)} %get-tuple-element.331), channel_id=1, source_target_pairs={{0,4},{1,5},{2,6},{3,7},{4,0},{5,1},{6,2},{7,3},{8,12},{9,13},{10,... | collective-permute-start | bytes 2064392 | tf_op jit(solution)/shard_map/ppermute | solution.py:22
  408.2 11.5 %copy-start.4 = (pred[64,8]{1,0:T(8,128)(4,1)S(1)}, pred[64,8]{1,0:T(8,128)(4,1)}, u32[]{:S(2)}) copy-start(pred[64,8]{1,0:T(8,128)(4,1)} %copy.50) | copy-start | bytes 1540
  408.2 41.4 %copy-start.2 = (bf16[16,3584]{1,0:T(8,128)(2,1)S(1)}, bf16[16,3584]{1,0:T(8,128)(2,1)}, u32[]{:S(2)}) copy-start(bf16[16,3584]{1,0:T(8,128)(2,1)} %reduce-scatter.3.cloned.1.call-done) | copy-start | bytes 344068
Sparse Core Ops, SparseCore 0:
  71.6 34.3 reduce-scatter.2
  426.6 22.9 reduce-scatter.4
